TPU v7x, 128 devices: a whole 4x4x4 slice. The times are simulated.
128 devices in a mesh: sec: 4 (over y), dp: 8 (over x_hi, z), mp: 4 (over x_lo, core).
Axes of the slice: x: 4 (x_hi: 2, x_lo: 2; x = x_hi * 2 + x_lo), y: 4, z: 4, core: 2. Of those that a mesh axis runs over, the one named last changes fastest.
Arguments:
- patches: bfloat16 [320, 5120], P('dp'), may hold values from -6 to 6
- ln_gain: bfloat16 [1280], replicated, may hold values from 0.099609375 to 1.8984375
- ln_shift: bfloat16 [1280], replicated, may hold values from -3 to 3
- w_in: bfloat16 [5120, 5120], P('dp', ('sec', 'mp')), may hold values from -0.078125 to 0.078125
- b_in: bfloat16 [5120], P(('sec', 'mp')), may hold values from -3 to 3
- w_out: bfloat16 [5120, 8192], P(('sec', 'mp'), 'dp'), may hold values from -0.125 to 0.125
- b_out: bfloat16 [8192], P(('sec', 'mp')), may hold values from -3 to 3
- place: int32 [320], P('dp'), may hold values from 0 to 255, as said below
- image_counts: int32 [8], P('dp'), may hold values from 1 to 40, 128 in all
- text_rows: bfloat16 [2048, 8192], P('dp', ('sec', 'mp')), may hold values from -6 to 6
- segments: int32 [8, 256], P('dp'), may hold values from 0 to 3, never falling along the last dimension, each value on 1 to 128 neighbouring positions
- norm_gain: bfloat16 [2, 8192], replicated, may hold values from 0.099609375 to 1.8984375
- q_weight: bfloat16 [2, 8192, 4096], P(None, None, ('sec', 'mp'))
- kv_weight: bfloat16 [2, 2, 512, 8192], P(None, None, ('sec', 'mp'))
- o_weight: bfloat16 [2, 4096, 8192], P(None, ('sec', 'mp')), may hold values from -0.125 to 0.125
- grad_rows: bfloat16 [320, 8192], P('dp'), may hold values from -6 to 6
Outputs:
- final_rows: float32 [2048, 8192], P('dp', ('sec', 'mp'))
- patch_grads: float32 [320, 5120], P('dp')
Inputs may be any that keep to these rules, and one draw needn't show every extreme that they name: `place`: each owner's 40 entries are distinct token positions of its own packed sequence; only an owner's first image_counts entries are used. `image_counts`: the counts sum to 8 * (16) over all owners.
All inputs are finite; a program needn't handle non-finite values. No bound on the sum of `image_counts` on one device may be relied on, other than what follows from the above.
Results may differ from a plain program's by a relative error of at most 0.0055.
Values may be sent and summed in bfloat16 or wider, within the bound.
A program may use at most 128 MiB of HBM per device.

v0:
```python
import math
import jax
import jax.numpy as jnp
from jax import lax
from jax.sharding import PartitionSpec as P

D = 8192
HEAD_DIM = 128
ln_eps = 1e-06
rms_eps = 1e-06
rope_base = 1000000.0


def group_norm(patch_rows, ln_gain, ln_shift):
    row_count = patch_rows.shape[0]
    grouped = patch_rows.astype(jnp.float32).reshape(row_count, -1, ln_gain.shape[0])
    center = grouped - jnp.mean(grouped, axis=-1, keepdims=True)
    spread = jnp.mean(center * center, axis=-1, keepdims=True)
    scaled = center * lax.rsqrt(spread + ln_eps) * ln_gain.astype(jnp.float32) + ln_shift.astype(
        jnp.float32
    )
    return scaled.reshape(row_count, -1)


def gelu_exact(values):
    return jax.nn.gelu(values, approximate=False)


def rotate(values, positions):
    head_depth = values.shape[-1]
    half_depth = head_depth // 2
    inv_freq = rope_base ** (-2.0 * jnp.arange(half_depth, dtype=jnp.float32) / head_depth)
    angles = positions[:, None] * inv_freq[None, :]
    cosine = jnp.cos(angles)[:, None, :]
    sine_part = jnp.sin(angles)[:, None, :]
    first_half = values[..., :half_depth]
    second = values[..., half_depth:]
    return jnp.concatenate(
        [first_half * cosine - second * sine_part, second * cosine + first_half * sine_part],
        axis=-1,
    )


def doc_mask(segment_ids):
    token_index = jnp.arange(segment_ids.shape[0], dtype=jnp.int32)
    same_doc = segment_ids[:, None] == segment_ids[None, :]
    allowed = same_doc & (token_index[None, :] <= token_index[:, None])
    positions = jnp.sum(allowed.astype(jnp.int32), axis=1) - 1
    return (allowed, positions.astype(jnp.float32))


def attend(normed, allowed, positions, q_local, kv_local):
    token_count = normed.shape[0]
    queries = jnp.dot(normed, q_local, preferred_element_type=jnp.float32).reshape(
        token_count, -1, HEAD_DIM
    )
    key_value = jnp.einsum("td,kcd->tkc", normed, kv_local, preferred_element_type=jnp.float32)
    key_value = lax.all_gather(key_value, "mp", axis=2, tiled=True)
    key_rows = rotate(key_value[:, 0:1, :], positions)[:, 0, :].astype(jnp.bfloat16)
    value_rows = key_value[:, 1, :].astype(jnp.bfloat16)
    queries = rotate(queries, positions).astype(jnp.bfloat16)
    scores = jnp.einsum("thd,sd->hts", queries, key_rows, preferred_element_type=jnp.float32) * (
        1.0 / math.sqrt(HEAD_DIM)
    )
    scores = jnp.where(allowed[None], scores, -jnp.inf)
    row_max = jnp.max(scores, axis=-1, keepdims=True)
    exp_scores = jnp.exp(scores - row_max)
    attn_weights = (exp_scores / jnp.sum(exp_scores, axis=-1, keepdims=True)).astype(jnp.bfloat16)
    attended = jnp.einsum(
        "hts,sd->thd", attn_weights, value_rows, preferred_element_type=jnp.float32
    )
    return attended.astype(jnp.bfloat16).reshape(token_count, -1)


def gather_features(rows_local):
    return lax.all_gather(rows_local, ("sec", "mp"), axis=1, tiled=True)


def section_features(rows_local, gain_row, allowed, positions, q_local, kv_local, o_local):
    share = rows_local.shape[1]
    square_sums = lax.psum(jnp.sum(rows_local * rows_local, axis=1), ("sec", "mp"))
    factor = lax.rsqrt(square_sums / D + rms_eps)
    gain_local = lax.dynamic_slice_in_dim(
        gain_row, lax.axis_index(("sec", "mp")) * share, share, 0
    ).astype(jnp.float32)
    normed_local = (rows_local * factor[:, None] * gain_local[None, :]).astype(jnp.bfloat16)
    normed = gather_features(normed_local)
    attended = attend(normed, allowed, positions, q_local, kv_local)
    summed = lax.psum_scatter(
        lax.dot_general(
            o_local, attended, (((0,), (1,)), ((), ())), preferred_element_type=jnp.float32
        ),
        ("sec", "mp"),
        scatter_dimension=0,
        tiled=True,
    )
    return rows_local + summed.T


def merger_front(patch_rows, ln_gain, ln_shift, w_in_full, b_in, w_out_full, b_out):
    normed = group_norm(patch_rows, ln_gain, ln_shift).astype(jnp.bfloat16)
    pre_act = jnp.dot(normed, w_in_full, preferred_element_type=jnp.float32) + b_in.astype(
        jnp.float32
    )
    hidden_units = gelu_exact(pre_act).astype(jnp.bfloat16)
    partial_out = jnp.dot(hidden_units, w_out_full, preferred_element_type=jnp.float32)
    merged = lax.psum_scatter(
        partial_out, ("sec", "mp"), scatter_dimension=1, tiled=True
    ) + b_out.astype(jnp.float32)
    return (merged.astype(jnp.bfloat16), pre_act)


def merger_back(patch_rows, pre_act, hidden_grads, ln_gain, ln_shift, w_in_full):
    _, pull_gelu = jax.vjp(gelu_exact, pre_act)
    pre_grads = pull_gelu(hidden_grads)[0].astype(jnp.bfloat16)
    normed_grads = lax.dot_general(
        pre_grads, w_in_full, (((1,), (1,)), ((), ())), preferred_element_type=jnp.float32
    )
    normed_grads = lax.psum(normed_grads, ("sec", "mp"))
    _, pull_norm = jax.vjp(
        lambda values: group_norm(values, ln_gain, ln_shift), patch_rows.astype(jnp.float32)
    )
    return pull_norm(normed_grads)[0]


def local(
    patches,
    ln_gain,
    ln_shift,
    w_in,
    b_in,
    w_out,
    b_out,
    place,
    image_counts,
    text_rows,
    segments,
    norm_gain,
    q_weight,
    kv_weight,
    o_weight,
    grad_rows,
):
    w_in_full, w_out_full = (
        lax.all_gather(w_in, "dp", axis=0, tiled=True),
        lax.all_gather(w_out, "dp", axis=1, tiled=True),
    )
    slot_count = patches.shape[0]
    tokens = text_rows.shape[0]
    slot_index = jnp.arange(slot_count, dtype=jnp.int32)
    live_slot = slot_index < image_counts[0]
    slot_grads = jnp.where(live_slot[:, None], grad_rows, jnp.zeros_like(grad_rows))
    hidden_grads = lax.dot_general(
        slot_grads, w_out_full, (((1,), (1,)), ((), ())), preferred_element_type=jnp.float32
    )
    merged_local, pre_act = merger_front(
        patches, ln_gain, ln_shift, w_in_full, b_in, w_out_full, b_out
    )
    patch_grads = merger_back(patches, pre_act, hidden_grads, ln_gain, ln_shift, w_in_full)
    token_index = jnp.arange(tokens, dtype=jnp.int32)
    select = (place[:, None] == token_index[None, :]) & live_slot[:, None]
    is_image = jnp.any(select, axis=0)
    picked = lax.dot_general(
        select.astype(jnp.bfloat16),
        merged_local,
        (((0,), (0,)), ((), ())),
        preferred_element_type=jnp.float32,
    )
    start_rows = jnp.where(is_image[:, None], picked, text_rows.astype(jnp.float32)).astype(
        jnp.bfloat16
    )
    allowed, positions = doc_mask(segments[0])
    layer_count = q_weight.shape[0]
    current = start_rows.astype(jnp.float32)
    for layer_index in range(layer_count):
        current = section_features(
            current,
            norm_gain[layer_index],
            allowed,
            positions,
            q_weight[layer_index],
            kv_weight[layer_index],
            o_weight[layer_index],
        )
    return (current, patch_grads)


def solution(mesh):
    in_specs = (
        P("dp", None),
        P(),
        P(),
        P("dp", ("sec", "mp")),
        P(("sec", "mp")),
        P(("sec", "mp"), "dp"),
        P(("sec", "mp")),
        P("dp"),
        P("dp"),
        P("dp", ("sec", "mp")),
        P("dp", None),
        P(),
        P(None, None, ("sec", "mp")),
        P(None, None, ("sec", "mp"), None),
        P(None, ("sec", "mp"), None),
        P("dp", None),
    )
    out_specs = (P("dp", ("sec", "mp")), P("dp", None))
    return jax.shard_map(local, mesh=mesh, in_specs=in_specs, out_specs=out_specs, check_vma=False)
```

profile of v0, /device:TPU:0, one launch (start us, length us, event | category | flops | bytes accessed | tf_op | source)
XLA Modules:
  0.0 707.5 jit_solution(7781813747117255810)
XLA Ops:
  7.2 0.7 all-gather.5.cloned.1.call-update
  8.0 0.7 all-gather.7.cloned.1.call-update
  8.7 1.4 reshape.223
  10.4 0.4 multiply_reduce_fusion.1
  11.5 64.8 %all-gather.5.cloned.1.call-done = bf16[5120,320]{0,1:T(8,128)(2,1)} async-done(((bf16[640,320]{0,1:T(8,128)(2,1)}), bf16[5120,320]{0,1:T(8,128)(2,1)}) %all-gather.5.cloned.1.call-update) | async-done | bytes 3276816 | tf_op jit(solution)/shard_map/all_gather | solution.py:145
  76.3 3.0 convolution_add_fusion
  79.4 77.0 %all-gather.7.cloned.1.call-done = bf16[320,8192]{1,0:T(8,128)(2,1)} async-done(((bf16[320,1024]{1,0:T(8,128)(2,1)}), bf16[320,8192]{1,0:T(8,128)(2,1)}) %all-gather.7.cloned.1.call-update) | async-done | bytes 5242896 | tf_op jit(solution)/shard_map/all_gather | solution.py:146
  156.4 4.6 fusion.88
  162.0 60.0 %reduce-scatter.4.cloned.1.call-done = f32[40,512]{1,0:T(8,128)} async-done(((f32[40,8192]{1,0:T(8,128)}), f32[40,512]{1,0:T(8,128)}) %reduce-scatter.4.cloned.1.call-update) | async-done | bytes 81936 | tf_op jit(solution)/shard_map/reduce_scatter | solution.py:107
  222.0 1.4 multiply_reduce_fusion.3
  223.4 27.7 %psum.21 = f32[256]{0:T(256)S(1)} all-reduce(f32[256]{0:T(256)S(1)} %get-tuple-element.16), channel_id=1, replica_groups=mesh['sec'=4,'dp'=8,'mp'=4] {'sec','mp'}, use_global_device_ids=true, to_apply=%region_5.6 | all-reduce | flops 256 | bytes 2048 | tf_op jit(solution)/shard_map/psum | solution.py:81
  251.1 0.8 multiply_convert_fusion.1
  252.0 5.7 slice_bitcast_fusion.1
  257.8 6.4 copy.26
  264.5 0.3 multiply_cosine_fusion
  264.8 23.3 %all-gather.9.cloned.1.call-done = bf16[256,8192]{1,0:T(8,128)(2,1)} async-done(((bf16[256,512]{1,0:T(8,128)(2,1)}), bf16[256,8192]{1,0:T(8,128)(2,1)}) %all-gather.9.cloned.1.call-update) | async-done | bytes 4194320 | tf_op jit(solution)/shard_map/all_gather | solution.py:76
  288.1 4.0 fusion.10
  292.1 5.8 all_gather.21
  297.9 0.3 fusion.52
  298.3 3.5 fusion.8
  301.8 0.6 copy-done.12
  302.4 1.0 fusion.21
  303.5 1.2 fusion.117
  304.7 1.6 convolution_convert_fusion.1
  306.3 6.7 convolution_bitcast_fusion.1
  313.1 97.8 %reduce-scatter.6.cloned.1.call-done = f32[512,256]{0,1:T(8,128)} async-done(((f32[8192,256]{0,1:T(8,128)}), f32[512,256]{0,1:T(8,128)}) %reduce-scatter.6.cloned.1.call-update) | async-done | bytes 524304 | tf_op jit(solution)/shard_map/reduce_scatter | solution.py:89
  410.9 1.2 multiply_reduce_fusion.2
  412.1 27.6 %psum.22 = f32[256]{0:T(256)S(1)} all-reduce(f32[256]{0:T(256)S(1)} %multiply_reduce_fusion.2), channel_id=1, replica_groups=mesh['sec'=4,'dp'=8,'mp'=4] {'sec','mp'}, use_global_device_ids=true, to_apply=%region_11.12 | all-reduce | flops 256 | bytes 2048 | tf_op jit(solution)/shard_map/psum | solution.py:81
  439.7 1.9 multiply_convert_fusion
  441.8 6.5 copy.30
  448.3 7.6 %fusion.71 = f32[40,5120]{1,0:T(8,128)} fusion(bf16[5120,320]{0,1:T(8,128)(2,1)} %all-gather.5.cloned.1.call-done, bf16[320,8192]{1,0:T(8,128)(2,1)} %all-gather.7.cloned.1.call-done, bf16[40,8192]{1,0:T(8,128)(2,1)S(1)} %copy-done.7, pred[40]{0:T(512)(128)(4,1)S(1)} %iota_compare_fusion.2, f32[40,320]{1,0:T(8,128)S(1)} %convolution_add_fusion), kind=kOutput, calls=%fused_computation.107 | convolution fusion | flops 342036480 | bytes 10045480 | tf_op jit(solution)/shard_map/dot_general | solution.py:116
  456.0 21.5 %all-gather.11.cloned.1.call-done = bf16[256,8192]{1,0:T(8,128)(2,1)} async-done(((bf16[256,512]{1,0:T(8,128)(2,1)}), bf16[256,8192]{1,0:T(8,128)(2,1)}) %all-gather.11.cloned.1.call-update) | async-done | bytes 4194320 | tf_op jit(solution)/shard_map/all_gather | solution.py:76
  477.5 4.0 fusion.5
  481.5 5.8 all_gather.23
  487.3 0.3 fusion.56
  487.6 3.5 fusion.3
  491.2 0.6 copy-done.11
  491.8 1.0 fusion.19
  492.9 1.2 fusion.120
  494.1 1.6 convolution_convert_fusion
  495.7 6.7 convolution_bitcast_fusion
  502.4 97.3 %all-reduce.2.cloned.1.call-done = f32[40,5120]{1,0:T(8,128)} async-done(((f32[40,5120]{1,0:T(8,128)}), f32[40,5120]{1,0:T(8,128)}) %all-reduce.2.cloned.1.call-update) | async-done | bytes 819216 | tf_op jit(solution)/shard_map/psum | solution.py:119
  599.7 1.5 reshape.226
  601.3 0.4 multiply_reduce_fusion
  601.7 0.6 fusion.29
  603.0 1.2 fusion.28
  604.2 94.5 %reduce-scatter.8.cloned.1.call-done = f32[512,256]{0,1:T(8,128)} async-done(((f32[8192,256]{0,1:T(8,128)}), f32[512,256]{0,1:T(8,128)}) %reduce-scatter.8.cloned.1.call-update) | async-done | bytes 524304 | tf_op jit(solution)/shard_map/reduce_scatter | solution.py:89
  698.7 2.0 bitcast_add_fusion
  (87 shorter events, 2.8 us)
Async XLA Ops:
  7.2 69.2 %all-gather.5.cloned.1.call-start = ((), (), s32[]{:S(2)}) async-start(), calls=%async_computation.3 | async-start | bytes 3686400 | tf_op jit(solution)/shard_map/all_gather | solution.py:145
  7.9 3.5 copy-start.16
  7.9 3.6 copy-start.17
  7.9 148.5 %all-gather.7.cloned.1.call-start = ((), (), s32[]{:S(2)}) async-start(), calls=%async_computation.4 | async-start | bytes 5898240 | tf_op jit(solution)/shard_map/all_gather | solution.py:146
  8.7 2.8 copy-start.18
  8.7 67.7 %copy-start.5 = (bf16[40,5120]{1,0:T(8,128)(2,1)S(1)}, bf16[40,5120]{1,0:T(8,128)(2,1)}, u32[]{:S(2)}) copy-start(bf16[40,5120]{1,0:T(8,128)(2,1)} %param.16) | copy-start | bytes 1228804
  8.7 213.3 %reduce-scatter.4.cloned.1.call-start = ((), (), s32[]{:S(2)}) async-start(), calls=%async_computation.5 | async-start | bytes 1392640 | tf_op jit(solution)/shard_map/reduce_scatter | solution.py:107
  11.4 149.7 %copy-start = (f32[5,8,4,1280]{3,1,2,0:T(8,128)}, f32[5,8,4,1280]{3,1,2,0:T(8,128)S(1)}, u32[]{:S(2)}) copy-start(f32[5,8,4,1280]{3,1,2,0:T(8,128)S(1)} %copy.42) | copy-start | bytes 2457604
  79.4 82.4 %copy-start.19 = (bf16[512]{0:T(512)(128)(2,1)S(1)}, bf16[512]{0:T(512)(128)(2,1)}, u32[]{:S(2)}) copy-start(bf16[512]{0:T(512)(128)(2,1)} %param.22) | copy-start | bytes 3076
  79.4 82.5 %copy-start.8 = (bf16[2,8192]{1,0:T(2,128)(2,1)S(1)}, bf16[2,8192]{1,0:T(2,128)(2,1)}, u32[]{:S(2)}) copy-start(bf16[2,8192]{1,0:T(2,128)(2,1)} %param.27) | copy-start | bytes 98308
  79.4 82.5 %copy-start.20 = (s32[40]{0:T(128)S(1)}, s32[40]{0:T(128)}, u32[]{:S(2)}) copy-start(s32[40]{0:T(128)} %param.23) | copy-start | bytes 484
  161.1 127.0 %all-gather.9.cloned.1.call-start = ((), (), s32[]{:S(2)}) async-start(), calls=%async_computation.6 | async-start | bytes 4456448 | tf_op jit(solution)/shard_map/all_gather | solution.py:76
  252.0 158.9 %reduce-scatter.6.cloned.1.call-start = ((), (), s32[]{:S(2)}) async-start(), calls=%async_computation.7 | async-start | bytes 8912896 | tf_op jit(solution)/shard_map/reduce_scatter | solution.py:89
  257.8 6.4 copy-start.15
  264.4 39.0 %copy-start.9 = (pred[256,256]{0,1:T(8,128)(4,1)}, pred[256,256]{0,1:T(8,128)(4,1)S(1)}, u32[]{:S(2)}) copy-start(pred[256,256]{0,1:T(8,128)(4,1)S(1)} %fusion.36) | copy-start | bytes 196612
  288.1 10.2 %copy-start.4 = (bf16[256,8192]{1,0:T(8,128)(2,1)S(1)}, bf16[256,8192]{1,0:T(8,128)(2,1)}, u32[]{:S(2)}) copy-start(bf16[256,8192]{1,0:T(8,128)(2,1)} %copy.26) | copy-start | bytes 12582916
  298.2 3.6 copy-start.13
  298.2 3.6 copy-start.14
  301.8 0.6 copy-start.12
  313.0 164.4 %all-gather.11.cloned.1.call-start = ((), (), s32[]{:S(2)}) async-start(), calls=%async_computation.8 | async-start | bytes 4456448 | tf_op jit(solution)/shard_map/all_gather | solution.py:76
  441.6 158.2 %all-reduce.2.cloned.1.call-start = ((), (), s32[]{:S(2)}) async-start(), calls=%async_computation.10 | async-start | bytes 1638400 | tf_op jit(solution)/shard_map/psum | solution.py:119
  441.8 6.5 copy-start.7
  455.9 242.8 %reduce-scatter.8.cloned.1.call-start = ((), (), s32[]{:S(2)}) async-start(), calls=%async_computation.9 | async-start | bytes 8912896 | tf_op jit(solution)/shard_map/reduce_scatter | solution.py:89
  477.5 10.1 %copy-start.3 = (bf16[256,8192]{1,0:T(8,128)(2,1)S(1)}, bf16[256,8192]{1,0:T(8,128)(2,1)}, u32[]{:S(2)}) copy-start(bf16[256,8192]{1,0:T(8,128)(2,1)} %copy.30) | copy-start | bytes 12582916
  487.6 4.2 copy-start.10
  491.2 0.6 copy-start.11
  601.3 1.7 copy-start.1
  601.3 1.7 copy-start.6
  602.6 96.1 %copy-start.2 = (f32[512,256]{0,1:T(8,128)S(1)}, f32[512,256]{0,1:T(8,128)}, u32[]{:S(2)}) copy-start(f32[512,256]{0,1:T(8,128)} %reduce-scatter.6.cloned.1.call-done) | copy-start | bytes 1572868
Sparse Core Ops, SparseCore 0:
  10.4 65.9 all-gather.4
  78.6 77.7 all-gather.6
  161.2 60.7 reduce-scatter.3
  252.1 35.9 all-gather.8
  313.2 97.6 reduce-scatter.5
  441.7 35.7 all-gather.10
  480.5 119.1 all-reduce.1
  602.1 96.5 reduce-scatter.7
where the time goes:
time: 709 us; the launch traced here: 708 us
  waiting for transfers between devices  538 us (76%)
  blocking collectives  66.9 us (9%)
  matrix products  52.9 us (7%)
  local copies, waits for them, and re-layouts  24.3 us (3%)
  between operations  15.3 us (2%)
  other arithmetic  9.97 us (1%)
    reduce_scatter x2, waiting for transfers between devices, section_features(): lax.psum_scatter(lax.dot_general(o_local, attended, (((0,), (1,)), ((), (...  192 us
    psum x1, waiting for transfers between devices, merger_back(): normed_grads = lax.psum(normed_grads, ('sec', 'mp'))  97.3 us
    all_gather x1, waiting for transfers between devices, local(): lax.all_gather(w_out, 'dp', axis=1, tiled=True)  77 us
    all_gather x1, waiting for transfers between devices, local(): lax.all_gather(w_in, 'dp', axis=0, tiled=True)  64.8 us
    reduce_scatter x1, waiting for transfers between devices, merger_front(): lax.psum_scatter(partial_out, ('sec', 'mp'), scatter_dimension=1, tiled=T...  60 us
    psum x2, blocking collectives, section_features(): lax.psum(jnp.sum(rows_local * rows_local, axis=1), ('sec', 'mp'))  55.3 us
    all_gather x2, waiting for transfers between devices, gather_features(): return lax.all_gather(rows_local, ('sec', 'mp'), axis=1, tiled=True)  44.8 us
    dot_general x3, local copies, waits for them, and re-layouts, attend(): jnp.dot(normed, q_local, preferred_element_type=jnp.float32)  18.6 us
  transfers between devices with their start and end apart: 8, of which 8 were waited for; matrix products, arithmetic and copies ran while one was open for 8% of the time, Pallas kernels for 0%

commit v1 on v0

--- a/solution.py
+++ b/solution.py
@@ -78,7 +78,8 @@
 
 def section_features(rows_local, gain_row, allowed, positions, q_local, kv_local, o_local):
     share = rows_local.shape[1]
-    square_sums = lax.psum(jnp.sum(rows_local * rows_local, axis=1), ("sec", "mp"))
+    shard_in = jnp.sum(rows_local * rows_local, axis=1)
+    square_sums = jnp.sum(jax.lax.all_gather(shard_in, ("sec", "mp")), 0)
     factor = lax.rsqrt(square_sums / D + rms_eps)
     gain_local = lax.dynamic_slice_in_dim(
         gain_row, lax.axis_index(("sec", "mp")) * share, share, 0

time: 709 us -> 686 us (0.968)
  blocking collectives: 66.9 us -> 44.1 us
    psum x2 -> x0, blocking collectives: 55.3 us -> none  [section_features(): lax.psum(jnp.sum(rows_local * rows_local, axis=1), ('sec', 'mp'))]
    all_gather x0 -> x2, blocking collectives: none -> 32.5 us  [section_features(): square_sums = jnp.sum(jax.lax.all_gather(shard_in, ('sec', 'mp')), 0)]
where the time goes in v1:
time: 686 us; the launch traced here: 685 us
  waiting for transfers between devices  538 us (78%)
  matrix products  52.9 us (8%)
  blocking collectives  44.1 us (6%)
  local copies, waits for them, and re-layouts  24.3 us (4%)
  between operations  15.3 us (2%)
  other arithmetic  10 us (1%)
    reduce_scatter x2, waiting for transfers between devices, section_features(): lax.psum_scatter(lax.dot_general(o_local, attended, (((0,), (1,)), ((), (...  192 us
    psum x1, waiting for transfers between devices, merger_back(): normed_grads = lax.psum(normed_grads, ('sec', 'mp'))  97.2 us
    all_gather x1, waiting for transfers between devices, local(): lax.all_gather(w_out, 'dp', axis=1, tiled=True)  77 us
    all_gather x1, waiting for transfers between devices, local(): lax.all_gather(w_in, 'dp', axis=0, tiled=True)  64.8 us
    reduce_scatter x1, waiting for transfers between devices, merger_front(): lax.psum_scatter(partial_out, ('sec', 'mp'), scatter_dimension=1, tiled=T...  60 us
    all_gather x2, waiting for transfers between devices, gather_features(): return lax.all_gather(rows_local, ('sec', 'mp'), axis=1, tiled=True)  45.3 us
    all_gather x2, blocking collectives, section_features(): square_sums = jnp.sum(jax.lax.all_gather(shard_in, ('sec', 'mp')), 0)  32.5 us
    dot_general x3, local copies, waits for them, and re-layouts, attend(): jnp.dot(normed, q_local, preferred_element_type=jnp.float32)  18.6 us
  transfers between devices with their start and end apart: 8, of which 8 were waited for; matrix products, arithmetic and copies ran while one was open for 8% of the time, Pallas kernels for 0%

profile of v1, /device:TPU:0, one launch (start us, length us, event | category | flops | bytes accessed | tf_op | source)
XLA Modules:
  0.0 685.3 jit_solution(261869376354673570)
XLA Ops:
  7.2 0.7 all-gather.9.cloned.1.call-update
  8.0 0.7 all-gather.11.cloned.1.call-update
  8.7 1.4 reshape.231
  10.4 0.4 multiply_reduce_fusion.1
  11.5 64.8 %all-gather.9.cloned.1.call-done = bf16[5120,320]{0,1:T(8,128)(2,1)} async-done(((bf16[640,320]{0,1:T(8,128)(2,1)}), bf16[5120,320]{0,1:T(8,128)(2,1)}) %all-gather.9.cloned.1.call-update) | async-done | bytes 3276816 | tf_op jit(solution)/shard_map/all_gather | solution.py:146
  76.3 3.0 convolution_add_fusion
  79.4 77.0 %all-gather.11.cloned.1.call-done = bf16[320,8192]{1,0:T(8,128)(2,1)} async-done(((bf16[320,1024]{1,0:T(8,128)(2,1)}), bf16[320,8192]{1,0:T(8,128)(2,1)}) %all-gather.11.cloned.1.call-update) | async-done | bytes 5242896 | tf_op jit(solution)/shard_map/all_gather | solution.py:147
  156.4 4.6 fusion.88
  162.0 60.0 %reduce-scatter.4.cloned.1.call-done = f32[40,512]{1,0:T(8,128)} async-done(((f32[40,8192]{1,0:T(8,128)}), f32[40,512]{1,0:T(8,128)}) %reduce-scatter.4.cloned.1.call-update) | async-done | bytes 81936 | tf_op jit(solution)/shard_map/reduce_scatter | solution.py:108
  222.0 1.4 multiply_reduce_fusion.3
  223.4 16.0 %all-gather.2 = f32[16,1,256]{2,1,0:T(1,128)S(1)} all-gather(f32[1,1,256]{2,1,0:T(1,128)S(1)} %bitcast.137), channel_id=2, replica_groups=mesh['sec'=4,'dp'=8,'mp'=4] {'sec','mp'}, dimensions={0}, use_global_device_ids=true | all-gather | bytes 17408 | tf_op jit(solution)/shard_map/all_gather | solution.py:82
  239.5 0.8 multiply_convert_fusion.1
  240.4 5.7 slice_bitcast_fusion.1
  246.1 6.4 copy.34
  252.8 0.3 multiply_cosine_fusion
  253.1 23.6 %all-gather.13.cloned.1.call-done = bf16[256,8192]{1,0:T(8,128)(2,1)} async-done(((bf16[256,512]{1,0:T(8,128)(2,1)}), bf16[256,8192]{1,0:T(8,128)(2,1)}) %all-gather.13.cloned.1.call-update) | async-done | bytes 4194320 | tf_op jit(solution)/shard_map/all_gather | solution.py:76
  276.7 4.0 fusion.10
  280.7 5.8 all_gather.35
  286.5 0.3 fusion.52
  286.9 3.5 fusion.8
  290.4 0.6 copy-done.12
  291.0 1.1 fusion.21
  292.1 1.2 fusion.117
  293.3 1.6 convolution_convert_fusion.1
  294.9 6.7 convolution_bitcast_fusion.1
  301.7 97.8 %reduce-scatter.6.cloned.1.call-done = f32[512,256]{0,1:T(8,128)} async-done(((f32[8192,256]{0,1:T(8,128)}), f32[512,256]{0,1:T(8,128)}) %reduce-scatter.6.cloned.1.call-update) | async-done | bytes 524304 | tf_op jit(solution)/shard_map/reduce_scatter | solution.py:90
  399.5 1.2 multiply_reduce_fusion.2
  400.7 16.5 %all-gather.3 = f32[16,1,256]{2,1,0:T(1,128)S(1)} all-gather(f32[1,1,256]{2,1,0:T(1,128)S(1)} %bitcast.138), channel_id=3, replica_groups=mesh['sec'=4,'dp'=8,'mp'=4] {'sec','mp'}, dimensions={0}, use_global_device_ids=true | all-gather | bytes 17408 | tf_op jit(solution)/shard_map/all_gather | solution.py:82
  417.3 1.9 multiply_convert_fusion
  419.4 6.5 copy.38
  425.8 7.6 %fusion.71 = f32[40,5120]{1,0:T(8,128)} fusion(bf16[5120,320]{0,1:T(8,128)(2,1)} %all-gather.9.cloned.1.call-done, bf16[320,8192]{1,0:T(8,128)(2,1)} %all-gather.11.cloned.1.call-done, bf16[40,8192]{1,0:T(8,128)(2,1)S(1)} %copy-done.7, pred[40]{0:T(512)(128)(4,1)S(1)} %iota_compare_fusion.2, f32[40,320]{1,0:T(8,128)S(1)} %convolution_add_fusion), kind=kOutput, calls=%fused_computation.107 | convolution fusion | flops 342036480 | bytes 10045480 | tf_op jit(solution)/shard_map/dot_general | solution.py:117
  433.5 21.7 %all-gather.15.cloned.1.call-done = bf16[256,8192]{1,0:T(8,128)(2,1)} async-done(((bf16[256,512]{1,0:T(8,128)(2,1)}), bf16[256,8192]{1,0:T(8,128)(2,1)}) %all-gather.15.cloned.1.call-update) | async-done | bytes 4194320 | tf_op jit(solution)/shard_map/all_gather | solution.py:76
  455.3 4.0 fusion.5
  459.3 5.8 all_gather.39
  465.1 0.3 fusion.56
  465.4 3.5 fusion.3
  469.0 0.6 copy-done.11
  469.6 1.0 fusion.19
  470.7 1.2 fusion.120
  471.9 1.6 convolution_convert_fusion
  473.5 6.7 convolution_bitcast_fusion
  480.2 97.2 %all-reduce.2.cloned.1.call-done = f32[40,5120]{1,0:T(8,128)} async-done(((f32[40,5120]{1,0:T(8,128)}), f32[40,5120]{1,0:T(8,128)}) %all-reduce.2.cloned.1.call-update) | async-done | bytes 819216 | tf_op jit(solution)/shard_map/psum | solution.py:120
  577.5 1.5 reshape.234
  579.1 0.4 multiply_reduce_fusion
  579.5 0.6 fusion.29
  580.7 1.2 fusion.28
  581.9 94.5 %reduce-scatter.8.cloned.1.call-done = f32[512,256]{0,1:T(8,128)} async-done(((f32[8192,256]{0,1:T(8,128)}), f32[512,256]{0,1:T(8,128)}) %reduce-scatter.8.cloned.1.call-update) | async-done | bytes 524304 | tf_op jit(solution)/shard_map/reduce_scatter | solution.py:90
  676.5 2.0 bitcast_add_fusion
  (89 shorter events, 2.8 us)
Async XLA Ops:
  7.2 69.2 %all-gather.9.cloned.1.call-start = ((), (), s32[]{:S(2)}) async-start(), calls=%async_computation.3 | async-start | bytes 3686400 | tf_op jit(solution)/shard_map/all_gather | solution.py:146
  7.9 3.5 copy-start.16
  7.9 3.6 copy-start.17
  7.9 148.5 %all-gather.11.cloned.1.call-start = ((), (), s32[]{:S(2)}) async-start(), calls=%async_computation.4 | async-start | bytes 5898240 | tf_op jit(solution)/shard_map/all_gather | solution.py:147
  8.7 2.8 copy-start.18
  8.7 67.7 %copy-start.5 = (bf16[40,5120]{1,0:T(8,128)(2,1)S(1)}, bf16[40,5120]{1,0:T(8,128)(2,1)}, u32[]{:S(2)}) copy-start(bf16[40,5120]{1,0:T(8,128)(2,1)} %param.16) | copy-start | bytes 1228804
  8.7 213.3 %reduce-scatter.4.cloned.1.call-start = ((), (), s32[]{:S(2)}) async-start(), calls=%async_computation.5 | async-start | bytes 1392640 | tf_op jit(solution)/shard_map/reduce_scatter | solution.py:108
  11.4 149.7 %copy-start = (f32[5,8,4,1280]{3,1,2,0:T(8,128)}, f32[5,8,4,1280]{3,1,2,0:T(8,128)S(1)}, u32[]{:S(2)}) copy-start(f32[5,8,4,1280]{3,1,2,0:T(8,128)S(1)} %copy.50) | copy-start | bytes 2457604
  79.4 82.4 %copy-start.19 = (bf16[512]{0:T(512)(128)(2,1)S(1)}, bf16[512]{0:T(512)(128)(2,1)}, u32[]{:S(2)}) copy-start(bf16[512]{0:T(512)(128)(2,1)} %param.22) | copy-start | bytes 3076
  79.4 82.5 %copy-start.8 = (bf16[2,8192]{1,0:T(2,128)(2,1)S(1)}, bf16[2,8192]{1,0:T(2,128)(2,1)}, u32[]{:S(2)}) copy-start(bf16[2,8192]{1,0:T(2,128)(2,1)} %param.27) | copy-start | bytes 98308
  79.4 82.5 %copy-start.20 = (s32[40]{0:T(128)S(1)}, s32[40]{0:T(128)}, u32[]{:S(2)}) copy-start(s32[40]{0:T(128)} %param.23) | copy-start | bytes 484
  161.1 115.6 %all-gather.13.cloned.1.call-start = ((), (), s32[]{:S(2)}) async-start(), calls=%async_computation.6 | async-start | bytes 4456448 | tf_op jit(solution)/shard_map/all_gather | solution.py:76
  240.3 159.2 %reduce-scatter.6.cloned.1.call-start = ((), (), s32[]{:S(2)}) async-start(), calls=%async_computation.7 | async-start | bytes 8912896 | tf_op jit(solution)/shard_map/reduce_scatter | solution.py:90
  246.1 6.4 copy-start.15
  252.8 39.3 %copy-start.9 = (pred[256,256]{0,1:T(8,128)(4,1)}, pred[256,256]{0,1:T(8,128)(4,1)S(1)}, u32[]{:S(2)}) copy-start(pred[256,256]{0,1:T(8,128)(4,1)S(1)} %fusion.36) | copy-start | bytes 196612
  276.7 10.2 %copy-start.4 = (bf16[256,8192]{1,0:T(8,128)(2,1)S(1)}, bf16[256,8192]{1,0:T(8,128)(2,1)}, u32[]{:S(2)}) copy-start(bf16[256,8192]{1,0:T(8,128)(2,1)} %copy.34) | copy-start | bytes 12582916
  286.8 3.6 copy-start.13
  286.8 3.6 copy-start.14
  290.4 0.6 copy-start.12
  301.7 153.6 %all-gather.15.cloned.1.call-start = ((), (), s32[]{:S(2)}) async-start(), calls=%async_computation.8 | async-start | bytes 4456448 | tf_op jit(solution)/shard_map/all_gather | solution.py:76
  419.1 158.3 %all-reduce.2.cloned.1.call-start = ((), (), s32[]{:S(2)}) async-start(), calls=%async_computation.10 | async-start | bytes 1638400 | tf_op jit(solution)/shard_map/psum | solution.py:120
  419.4 6.5 copy-start.7
  433.5 243.0 %reduce-scatter.8.cloned.1.call-start = ((), (), s32[]{:S(2)}) async-start(), calls=%async_computation.9 | async-start | bytes 8912896 | tf_op jit(solution)/shard_map/reduce_scatter | solution.py:90
  455.3 10.1 %copy-start.3 = (bf16[256,8192]{1,0:T(8,128)(2,1)S(1)}, bf16[256,8192]{1,0:T(8,128)(2,1)}, u32[]{:S(2)}) copy-start(bf16[256,8192]{1,0:T(8,128)(2,1)} %copy.38) | copy-start | bytes 12582916
  465.4 4.2 copy-start.10
  469.0 0.6 copy-start.11
  579.0 1.7 copy-start.1
  579.0 1.7 copy-start.6
  580.4 96.1 %copy-start.2 = (f32[512,256]{0,1:T(8,128)S(1)}, f32[512,256]{0,1:T(8,128)}, u32[]{:S(2)}) copy-start(f32[512,256]{0,1:T(8,128)} %reduce-scatter.6.cloned.1.call-done) | copy-start | bytes 1572868
Sparse Core Ops, SparseCore 0:
  10.4 65.9 all-gather.8
  78.6 77.7 all-gather.10
  161.2 60.7 reduce-scatter.3
  240.4 36.2 all-gather.12
  301.8 97.6 reduce-scatter.5
  419.3 35.9 all-gather.14
  458.3 119.0 all-reduce.1
  579.9 96.5 reduce-scatter.7
